TPU v7x, 32 devices: a whole 2x2x4 slice. The times are simulated.
32 devices in a mesh: fsdp: 2 (over y), ctx: 4 (over x, core), tp: 4 (over z).
Axes of the slice: x: 2, y: 2, z: 4, core: 2. Of those that a mesh axis runs over, the one named last changes fastest.
Arguments:
- inputs: bfloat16 [4, 2048, 768], P('fsdp', 'ctx'), may hold values from -6 to 6
- segment_ids: int32 [4, 2048], P('fsdp'), may hold values from 0 to 31, never falling along the last dimension, each value on 1 to 1025 neighbouring positions
- query_weight: float32 [768, 768], P(('fsdp', 'ctx'), 'tp'), may hold values from -0.3125 to 0.3125
- query_bias: float32 [768], P('tp'), may hold values from -3 to 3
- key_weight: float32 [768, 768], P(('fsdp', 'ctx'), 'tp'), may hold values from -0.3125 to 0.3125
- value_weight: float32 [768, 768], P(('fsdp', 'ctx'), 'tp'), may hold values from -0.21875 to 0.21875
- value_bias: float32 [768], P('tp'), may hold values from -3 to 3
- output_weight: float32 [768, 768], P('tp', ('fsdp', 'ctx')), may hold values from -0.875 to 0.875
- output_bias: float32 [768], replicated, may hold values from -3 to 3
- first_gain: float32 [768], replicated, may hold values from 0.5 to 1.5
- first_shift: float32 [768], replicated, may hold values from -2 to 2
- up_weight: float32 [768, 3072], P(('fsdp', 'ctx'), 'tp'), may hold values from -0.21875 to 0.21875
- up_bias: float32 [3072], P('tp'), may hold values from -3 to 3
- down_weight: float32 [3072, 768], P('tp', ('fsdp', 'ctx')), may hold values from -0.109375 to 0.109375
- down_bias: float32 [768], replicated, may hold values from -3 to 3
- second_gain: float32 [768], replicated, may hold values from 0.5 to 1.5
- second_shift: float32 [768], replicated, may hold values from -2 to 2
- cotangent: bfloat16 [4, 2048, 768], P('fsdp', 'ctx'), may hold values from -6 to 6
Outputs:
- layer_output: bfloat16 [4, 2048, 768], P('fsdp', 'ctx')
- input_grad: bfloat16 [4, 2048, 768], P('fsdp', 'ctx')
- query_weight_grad: float32 [768, 768], P(('fsdp', 'ctx'), 'tp')
- query_bias_grad: float32 [768], P('tp')
- key_weight_grad: float32 [768, 768], P(('fsdp', 'ctx'), 'tp')
- value_weight_grad: float32 [768, 768], P(('fsdp', 'ctx'), 'tp')
- value_bias_grad: float32 [768], P('tp')
- output_weight_grad: float32 [768, 768], P('tp', ('fsdp', 'ctx'))
- output_bias_grad: float32 [768], replicated
- first_gain_grad: float32 [768], replicated
- first_shift_grad: float32 [768], replicated
- up_weight_grad: float32 [768, 3072], P(('fsdp', 'ctx'), 'tp')
- up_bias_grad: float32 [3072], P('tp')
- down_weight_grad: float32 [3072, 768], P('tp', ('fsdp', 'ctx'))
- down_bias_grad: float32 [768], replicated
- second_gain_grad: float32 [768], replicated
- second_shift_grad: float32 [768], replicated
Inputs may be any that keep to these rules, and one draw needn't show every extreme that they name: `segment_ids`: along a sequence the document numbers never fall; every number appears, a document holds 1 to 1025 tokens and in every sequence some document holds exactly 1025.
All inputs are finite; a program needn't handle non-finite values.
Results may differ from a plain program's by a relative error of at most 0.015.
The roundings to bfloat16 on the way count: a program that leaves them out, or rounds other values in their place, can miss the bound.
Values may be sent and summed in bfloat16 or wider, within the bound.
No kernel may reach another device: no remote copies, remote signals or barrier semaphores. Data moves between devices by JAX's collectives and lax.ppermute only.
A program may use at most 128 MiB of HBM per device.

v0:
```python
import math
import jax
import jax.numpy as jnp
from jax import lax
from jax.sharding import PartitionSpec as P

DH = 64
EPSILON = 1e-05
MASKED = -1e30
ROOT_HALF = 0.7071067811865476
ROOT_TWO_PI = 2.5066282746310002


def matmul(left, right):
    return jnp.dot(left, right, preferred_element_type=jnp.float32)


def inner_rows(left, right):
    return lax.dot_general(
        left, right, (((0,), (0,)), ((), ())), preferred_element_type=jnp.float32
    )


def outer_rows(left, right):
    return lax.dot_general(
        left, right, (((1,), (1,)), ((), ())), preferred_element_type=jnp.float32
    )


def head_total(partial_value):
    return lax.psum(partial_value, "tp")


def head_major(flat_rows, seq_count, rows, heads_local):
    return flat_rows.reshape(seq_count, rows, heads_local, DH).transpose(0, 2, 1, 3)


def token_major(heads_first):
    seq_count, heads_local, rows, size = heads_first.shape
    return heads_first.transpose(0, 2, 1, 3).reshape(seq_count * rows, heads_local * size)


def normalize(resid, gain, shift):
    center = resid - jnp.mean(resid, axis=-1, keepdims=True)
    inverse = lax.rsqrt(jnp.mean(center * center, axis=-1, keepdims=True) + EPSILON)
    normed = center * inverse
    return (normed * gain + shift, normed, inverse)


def norm_back(grad, normed, inverse, gain):
    scaled = grad * gain
    inner = (
        scaled
        - jnp.mean(scaled, axis=-1, keepdims=True)
        - normed * jnp.mean(scaled * normed, axis=-1, keepdims=True)
    )
    return (inner * inverse, jnp.sum(grad * normed, axis=0), jnp.sum(grad, axis=0))


def scores_of(query_seq, key_seq, query_docs, key_docs):
    raw = jnp.einsum("hqd,hkd->hqk", query_seq, key_seq, preferred_element_type=jnp.float32) * (
        1.0 / math.sqrt(DH)
    )
    allowed = query_docs[:, None] == key_docs[None, :]
    return jnp.where(allowed[None, :, :], raw, MASKED)


def attend_forward(item):
    query_seq, key_seq, value_seq, query_docs, key_docs = item
    masked = scores_of(query_seq, key_seq, query_docs, key_docs)
    top = jnp.max(masked, axis=-1, keepdims=True)
    powers = jnp.exp(masked - top)
    total = jnp.sum(powers, axis=-1, keepdims=True)
    weights = (powers / total).astype(jnp.bfloat16)
    mixed = jnp.einsum("hqk,hkd->hqd", weights, value_seq, preferred_element_type=jnp.float32)
    return (mixed.astype(jnp.bfloat16), top, total)


def attend_backward(item):
    query_seq, key_seq, value_seq, query_docs, key_docs, top, total, grad_mixed = item
    masked = scores_of(query_seq, key_seq, query_docs, key_docs)
    weights = jnp.exp(masked - top) / total
    rounded = weights.astype(jnp.bfloat16)
    grad_weights = jnp.einsum(
        "hqd,hkd->hqk", grad_mixed, value_seq, preferred_element_type=jnp.float32
    )
    along = jnp.sum(weights * grad_weights, axis=-1, keepdims=True)
    grad_scores = (weights * (grad_weights - along)).astype(jnp.bfloat16)
    scale = 1.0 / math.sqrt(DH)
    grad_query = (
        jnp.einsum("hqk,hkd->hqd", grad_scores, key_seq, preferred_element_type=jnp.float32) * scale
    ).astype(jnp.bfloat16)
    grad_key = (
        jnp.einsum("hqk,hqd->hkd", grad_scores, query_seq, preferred_element_type=jnp.float32)
        * scale
    )
    grad_value = jnp.einsum("hqk,hqd->hkd", rounded, grad_mixed, preferred_element_type=jnp.float32)
    return (grad_query, grad_key, grad_value)


def body(
    inputs,
    segment_ids,
    query_weight,
    query_bias,
    key_weight,
    value_weight,
    value_bias,
    output_weight,
    output_bias,
    first_gain,
    first_shift,
    up_weight,
    up_bias,
    down_weight,
    down_bias,
    second_gain,
    second_shift,
    cotangent,
):
    masters = (query_weight, key_weight, value_weight, up_weight, output_weight, down_weight)
    lowered = tuple((master.astype(jnp.bfloat16) for master in masters))
    gathered = (
        lax.all_gather(lowered[0], ("fsdp", "ctx"), axis=0, tiled=True),
        lax.all_gather(lowered[1], ("fsdp", "ctx"), axis=0, tiled=True),
        lax.all_gather(lowered[2], ("fsdp", "ctx"), axis=0, tiled=True),
        lax.all_gather(lowered[3], ("fsdp", "ctx"), axis=0, tiled=True),
        lax.all_gather(lowered[4], ("fsdp", "ctx"), axis=1, tiled=True),
        lax.all_gather(lowered[5], ("fsdp", "ctx"), axis=1, tiled=True),
    )
    query_full, key_full, value_full, up_full, output_full, down_full = gathered
    seq_count, rows, width = inputs.shape
    heads_local = query_full.shape[1] // DH
    flat = inputs.reshape(seq_count * rows, width)
    queries = (matmul(flat, query_full) + query_bias).astype(jnp.bfloat16)
    keys_mine = head_major(
        matmul(flat, key_full).astype(jnp.bfloat16), seq_count, rows, heads_local
    )
    values_mine = head_major(
        (matmul(flat, value_full) + value_bias).astype(jnp.bfloat16), seq_count, rows, heads_local
    )
    place = lax.axis_index("ctx")
    query_docs = lax.dynamic_slice_in_dim(segment_ids, place * rows, rows, 1)
    key_heads, value_heads = (
        lax.all_gather(keys_mine, "ctx", axis=2, tiled=True),
        lax.all_gather(values_mine, "ctx", axis=2, tiled=True),
    )
    query_heads = head_major(queries, seq_count, rows, heads_local)
    mixed, top, total = lax.map(
        attend_forward, (query_heads, key_heads, value_heads, query_docs, segment_ids)
    )
    mixed_flat = token_major(mixed)
    branch = head_total(matmul(mixed_flat, output_full)) + output_bias
    inputs_wide = flat.astype(jnp.float32)
    first, normed_one, inverse_one = normalize(inputs_wide + branch, first_gain, first_shift)
    first_low = first.astype(jnp.bfloat16)
    upper = matmul(first_low, up_full) + up_bias
    cumulative = 0.5 * (1.0 + lax.erf(upper * ROOT_HALF))
    active = (upper * cumulative).astype(jnp.bfloat16)
    down = head_total(matmul(active, down_full)) + down_bias
    result, normed_two, inverse_two = normalize(first + down, second_gain, second_shift)
    layer_output = result.astype(jnp.bfloat16).reshape(seq_count, rows, width)
    again = (
        lax.all_gather(lowered[0], ("fsdp", "ctx"), axis=0, tiled=True),
        lax.all_gather(lowered[1], ("fsdp", "ctx"), axis=0, tiled=True),
        lax.all_gather(lowered[2], ("fsdp", "ctx"), axis=0, tiled=True),
        lax.all_gather(lowered[3], ("fsdp", "ctx"), axis=0, tiled=True),
        lax.all_gather(lowered[4], ("fsdp", "ctx"), axis=1, tiled=True),
        lax.all_gather(lowered[5], ("fsdp", "ctx"), axis=1, tiled=True),
    )
    query_back, key_back, value_back, up_back, output_back, down_back = again
    grad_out = cotangent.reshape(seq_count * rows, width).astype(jnp.float32)
    grad_two, grad_second_gain, grad_second_shift = norm_back(
        grad_out, normed_two, inverse_two, second_gain
    )
    grad_down = grad_two.astype(jnp.bfloat16)
    grad_down_bias = jnp.sum(grad_down.astype(jnp.float32), axis=0)
    grad_down_weight = inner_rows(active, grad_down)
    grad_active = outer_rows(grad_down, down_back)
    density = jnp.exp(-0.5 * upper * upper) / ROOT_TWO_PI
    grad_upper = (grad_active * (cumulative + upper * density)).astype(jnp.bfloat16)
    grad_up_bias = jnp.sum(grad_upper.astype(jnp.float32), axis=0)
    grad_up_weight = inner_rows(first_low, grad_upper)
    grad_first = grad_two + head_total(outer_rows(grad_upper, up_back))
    grad_one, grad_first_gain, grad_first_shift = norm_back(
        grad_first, normed_one, inverse_one, first_gain
    )
    grad_branch = grad_one.astype(jnp.bfloat16)
    grad_output_bias = jnp.sum(grad_branch.astype(jnp.float32), axis=0)
    grad_output_weight = inner_rows(mixed_flat, grad_branch)
    grad_mixed = head_major(
        outer_rows(grad_branch, output_back).astype(jnp.bfloat16), seq_count, rows, heads_local
    )
    grad_query, grad_key_part, grad_value_part = lax.map(
        attend_backward,
        (query_heads, key_heads, value_heads, query_docs, segment_ids, top, total, grad_mixed),
    )
    grad_key_mine, grad_value_mine = (
        lax.psum_scatter(
            grad_key_part.astype(jnp.bfloat16), "ctx", scatter_dimension=2, tiled=True
        ).astype(jnp.float32),
        lax.psum_scatter(
            grad_value_part.astype(jnp.bfloat16), "ctx", scatter_dimension=2, tiled=True
        ).astype(jnp.float32),
    )
    grad_query_low = token_major(grad_query)
    grad_key_low = token_major(grad_key_mine.astype(jnp.bfloat16))
    grad_value_low = token_major(grad_value_mine.astype(jnp.bfloat16))
    grad_query_weight = inner_rows(flat, grad_query_low)
    grad_key_weight = inner_rows(flat, grad_key_low)
    grad_value_weight = inner_rows(flat, grad_value_low)
    grad_query_bias = jnp.sum(grad_query_low.astype(jnp.float32), axis=0)
    grad_value_bias = jnp.sum(grad_value_low.astype(jnp.float32), axis=0)
    input_part = (
        outer_rows(grad_query_low, query_back)
        + outer_rows(grad_key_low, key_back)
        + outer_rows(grad_value_low, value_back)
    )
    grad_inputs = (
        (grad_one + head_total(input_part)).astype(jnp.bfloat16).reshape(seq_count, rows, width)
    )
    grad_weights = (
        lax.psum_scatter(grad_query_weight, ("fsdp", "ctx"), scatter_dimension=0, tiled=True),
        lax.psum_scatter(grad_key_weight, ("fsdp", "ctx"), scatter_dimension=0, tiled=True),
        lax.psum_scatter(grad_value_weight, ("fsdp", "ctx"), scatter_dimension=0, tiled=True),
        lax.psum_scatter(grad_up_weight, ("fsdp", "ctx"), scatter_dimension=0, tiled=True),
        lax.psum_scatter(grad_output_weight, ("fsdp", "ctx"), scatter_dimension=1, tiled=True),
        lax.psum_scatter(grad_down_weight, ("fsdp", "ctx"), scatter_dimension=1, tiled=True),
    )
    grad_small = lax.psum(
        (
            grad_query_bias,
            grad_value_bias,
            grad_output_bias,
            grad_first_gain,
            grad_first_shift,
            grad_up_bias,
            grad_down_bias,
            grad_second_gain,
            grad_second_shift,
        ),
        ("fsdp", "ctx"),
    )
    return (
        layer_output,
        grad_inputs,
        grad_weights[0],
        grad_small[0],
        grad_weights[1],
        grad_weights[2],
        grad_small[1],
        grad_weights[4],
        grad_small[2],
        grad_small[3],
        grad_small[4],
        grad_weights[3],
        grad_small[5],
        grad_weights[5],
        grad_small[6],
        grad_small[7],
        grad_small[8],
    )


def solution(mesh):
    in_specs = (
        P("fsdp", "ctx", None),
        P("fsdp", None),
        P(("fsdp", "ctx"), "tp"),
        P("tp"),
        P(("fsdp", "ctx"), "tp"),
        P(("fsdp", "ctx"), "tp"),
        P("tp"),
        P("tp", ("fsdp", "ctx")),
        P(),
        P(),
        P(),
        P(("fsdp", "ctx"), "tp"),
        P("tp"),
        P("tp", ("fsdp", "ctx")),
        P(),
        P(),
        P(),
        P("fsdp", "ctx", None),
    )
    out_specs = (
        P("fsdp", "ctx", None),
        P("fsdp", "ctx", None),
        P(("fsdp", "ctx"), "tp"),
        P("tp"),
        P(("fsdp", "ctx"), "tp"),
        P(("fsdp", "ctx"), "tp"),
        P("tp"),
        P("tp", ("fsdp", "ctx")),
        P(),
        P(),
        P(),
        P(("fsdp", "ctx"), "tp"),
        P("tp"),
        P("tp", ("fsdp", "ctx")),
        P(),
        P(),
        P(),
    )
    return jax.shard_map(body, mesh=mesh, in_specs=in_specs, out_specs=out_specs, check_vma=False)
```

profile of v0, /device:TPU:0, one launch (start us, length us, event | category | flops | bytes accessed | tf_op | source)
XLA Modules:
  0.0 1002.9 jit_solution(7115701397755225684)
XLA Ops:
  9.1 11.0 %all_gather.31 = bf16[768,192]{1,0:T(8,128)(2,1)S(1)} all-gather(bf16[96,192]{1,0:T(8,128)(2,1)S(1)} %convert_element_type.109), channel_id=1, replica_groups=mesh['fsdp'=2,'ctx'=4,'tp'=4] {'fsdp','ctx'}, dimensions={0}, use_global_device_ids=true | all-gather | bytes 331776 | tf_op jit(solution)/shard_map/all_gather | solution.py:125
  24.2 9.6 all_gather.33
  36.5 9.2 all_gather.30
  47.4 9.9 all_gather.35
  57.3 9.3 all-gather.7.cloned.1.call-done
  66.6 43.0 %while.28 = (s32[]{:T(128)}, bf16[2,3,512,64]{2,3,1,0:T(8,128)(2,1)S(1)}, f32[2,3,512,1]{2,1,3,0:T(4,128)S(1)}, f32[2,3,512,1]{2,1,3,0:T(4,128)S(1)}, s32[2,512]...) while((s32[]{:T(128)}, ...), condition=%wide.region_3.4_spmd, body=%wide.region_0.3_spmd.sunk | while | flops 844198912 | bytes 50301076 | solution.py:149
  67.3 7.1 fusion.131
  88.8 7.1 fusion.131
  114.9 119.7 %all-reduce.6.cloned.1.call-done = f32[1024,768]{1,0:T(8,128)} async-done(((f32[1024,768]{1,0:T(8,128)}), f32[1024,768]{1,0:T(8,128)}) %all-reduce.6.cloned.1.call-update) | async-done | bytes 3145744 | tf_op jit(solution)/shard_map/psum | solution.py:31
  253.2 116.3 %all-reduce.8.cloned.1.call-done = f32[1024,768]{1,0:T(8,128)} async-done(((f32[1024,768]{1,0:T(8,128)}), f32[1024,768]{1,0:T(8,128)}) %all-reduce.8.cloned.1.call-update) | async-done | bytes 3145744 | tf_op jit(solution)/shard_map/psum | solution.py:31
  386.2 120.2 %all-reduce.10.cloned.1.call-done = f32[1024,768]{1,0:T(8,128)} async-done(((f32[1024,768]{1,0:T(8,128)}), f32[1024,768]{1,0:T(8,128)}) %all-reduce.10.cloned.1.call-update) | async-done | bytes 3145744 | tf_op jit(solution)/shard_map/psum | solution.py:31
  516.7 50.9 %while.29 = (s32[]{:T(128)}, bf16[2,3,512,64]{2,3,1,0:T(8,128)(2,1)}, bf16[2,3,2048,64]{2,3,1,0:T(8,128)(2,1)}, bf16[2,3,2048,64]{2,3,1,0:T(8,128)(2,1)}, s32[2,...) while((s32[]{:T(128)}, ...), condition=%wide.region_17.18_spmd, body=%wide.region_15.17_spmd.sunk | while | flops 2046360064 | bytes 189550000 | solution.py:194
  522.9 7.7 multiply_reduce_fusion.7
  548.2 7.7 multiply_reduce_fusion.7
  574.5 20.4 %reduce-scatter.17.cloned.1.call-done = bf16[2,3,512,64]{2,3,1,0:T(8,128)(2,1)} async-done(((bf16[2,3,2048,64]{2,3,1,0:T(8,128)(2,1)}), bf16[2,3,512,64]{2,3,1,0:T(8,128)(2,1)}) %reduce-scatter.17.cloned.1.call-update) | async-done | bytes 393232 | tf_op jit(solution)/shard_map/reduce_scatter | solution.py:199
  597.2 28.7 %reduce-scatter.19.cloned.1.call-done = bf16[2,3,512,64]{2,3,1,0:T(8,128)(2,1)} async-done(((bf16[2,3,2048,64]{2,3,1,0:T(8,128)(2,1)}), bf16[2,3,512,64]{2,3,1,0:T(8,128)(2,1)}) %reduce-scatter.19.cloned.1.call-update) | async-done | bytes 393232 | tf_op jit(solution)/shard_map/reduce_scatter | solution.py:202
  653.3 10.6 %reduce-scatter.31.cloned.1.call-done = f32[96,192]{1,0:T(8,128)} async-done(((f32[768,192]{1,0:T(8,128)}), f32[96,192]{1,0:T(8,128)}) %reduce-scatter.31.cloned.1.call-update) | async-done | bytes 73744
  666.9 25.2 %all-reduce = (f32[192]{0:T(256)}, f32[192]{0:T(256)}, f32[768]{0:T(1024)}, f32[768]{0:T(1024)}, f32[768]{0:T(1024)}, /*index=5*/f32[768]{0:T(1024)}, f32[768]{0:T(1024)}, f32[768]{0:T(1024)}, f32[768]{0:T(1024)}) all-reduce(f32[192]{0:T(256)S(1)} %reduce_sum.184, ...), channel_id=1, replica_groups=mesh['fsdp'=2,'ctx'=4,'tp'=4] {'fsdp','ctx'}, use_global_device_ids=true, to_apply=%region_23.24 | all-reduce | flops 5760 | bytes 46080 | tf_op jit(solution)/shard_map/psum | solution.py:230
  692.1 95.4 %all-reduce.12.cloned.1.call-done = f32[1024,768]{1,0:T(8,128)} async-done(((f32[1024,768]{1,0:T(8,128)}), f32[1024,768]{1,0:T(8,128)}) %all-reduce.12.cloned.1.call-update) | async-done | bytes 3145744 | tf_op jit(solution)/shard_map/psum | solution.py:31
  790.8 42.0 %reduce-scatter.23.cloned.1.call-done = f32[768,96]{0,1:T(8,128)} async-done(((f32[768,768]{0,1:T(8,128)}), f32[768,96]{0,1:T(8,128)}) %reduce-scatter.23.cloned.1.call-update) | async-done | bytes 294928 | tf_op jit(solution)/shard_map/reduce_scatter | solution.py:228
  832.8 46.8 %reduce-scatter.21.cloned.1.call-done = f32[96,768]{1,0:T(8,128)} async-done(((f32[768,768]{1,0:T(8,128)}), f32[96,768]{1,0:T(8,128)}) %reduce-scatter.21.cloned.1.call-update) | async-done | bytes 294928 | tf_op jit(solution)/shard_map/reduce_scatter | solution.py:226
  879.6 38.6 %reduce-scatter.25.cloned.1.call-done = f32[96,192]{1,0:T(8,128)} async-done(((f32[768,192]{1,0:T(8,128)}), f32[96,192]{1,0:T(8,128)}) %reduce-scatter.25.cloned.1.call-update) | async-done | bytes 73744
  918.2 38.7 %reduce-scatter.29.cloned.1.call-done = f32[96,192]{1,0:T(8,128)} async-done(((f32[768,192]{1,0:T(8,128)}), f32[96,192]{1,0:T(8,128)}) %reduce-scatter.29.cloned.1.call-update) | async-done | bytes 73744
  957.0 38.6 %reduce-scatter.27.cloned.1.call-done = f32[96,192]{1,0:T(8,128)} async-done(((f32[768,192]{1,0:T(8,128)}), f32[96,192]{1,0:T(8,128)}) %reduce-scatter.27.cloned.1.call-update) | async-done | bytes 73744
  (274 shorter events, 166.2 us)
Async XLA Ops:
  8.0 26.5 %copy-start.3 = (bf16[2,512,768]{2,1,0:T(8,128)(2,1)S(1)}, bf16[2,512,768]{2,1,0:T(8,128)(2,1)}, u32[]{:S(2)}) copy-start(bf16[2,512,768]{2,1,0:T(8,128)(2,1)} %param.22) | copy-start | bytes 4718596
  8.0 26.4 %copy-start.51 = (f32[192]{0:T(256)S(1)}, f32[192]{0:T(256)}, u32[]{:S(2)}) copy-start(f32[192]{0:T(256)} %param.28) | copy-start | bytes 2308
  8.1 49.3 %all-gather.5.cloned.1.call-start = ((), (), s32[]{:S(2)}) async-start(), calls=%async_computation.8 | async-start | bytes 1966080 | tf_op jit(solution)/shard_map/all_gather | solution.py:145
  24.1 22.3 %copy-start.52 = (f32[192]{0:T(256)S(1)}, f32[192]{0:T(256)}, u32[]{:S(2)}) copy-start(f32[192]{0:T(256)} %param.25) | copy-start | bytes 2308
  24.1 42.5 %all-gather.7.cloned.1.call-start = ((), (), s32[]{:S(2)}) async-start(), calls=%async_computation.9 | async-start | bytes 1966080 | tf_op jit(solution)/shard_map/all_gather | solution.py:146
  35.5 21.8 %copy-start.27 = (s32[2,2048]{1,0:T(2,128)S(1)}, s32[2,2048]{1,0:T(2,128)}, u32[]{:S(2)}) copy-start(s32[2,2048]{1,0:T(2,128)} %param.23) | copy-start | bytes 49156
  36.3 198.3 %all-reduce.6.cloned.1.call-start = ((), (), s32[]{:S(2)}) async-start(), calls=%async_computation.10 | async-start | bytes 6291456 | tf_op jit(solution)/shard_map/psum | solution.py:31
  113.4 125.9 %all-gather.9.cloned.1.call-start = ((), (), s32[]{:S(2)}) async-start(), calls=%async_computation.11 | async-start | bytes 1327104 | tf_op jit(solution)/shard_map/all_gather | solution.py:127
  114.1 130.3 %all-gather.11.cloned.1.call-start = ((), (), s32[]{:S(2)}) async-start(), calls=%async_computation.12 | async-start | bytes 1327104 | tf_op jit(solution)/shard_map/all_gather | solution.py:129
  114.9 254.6 %all-reduce.8.cloned.1.call-start = ((), (), s32[]{:S(2)}) async-start(), calls=%async_computation.13 | async-start | bytes 6291456 | tf_op jit(solution)/shard_map/psum | solution.py:31
  237.5 273.9 %copy-start.1 = (f32[1024,768]{1,0:T(8,128)}, f32[1024,768]{1,0:T(8,128)S(1)}, u32[]{:S(2)}) copy-start(f32[1024,768]{1,0:T(8,128)S(1)} %get-tuple-element.254) | copy-start | bytes 9437188
  249.3 257.2 %all-reduce.10.cloned.1.call-start = ((), (), s32[]{:S(2)}) async-start(), calls=%async_computation.14 | async-start | bytes 6291456 | tf_op jit(solution)/shard_map/psum | solution.py:31
  386.2 208.8 %reduce-scatter.17.cloned.1.call-start = ((), (), s32[]{:S(2)}) async-start(), calls=%async_computation.15 | async-start | bytes 1966080 | tf_op jit(solution)/shard_map/reduce_scatter | solution.py:199
  567.6 58.3 %reduce-scatter.19.cloned.1.call-start = ((), (), s32[]{:S(2)}) async-start(), calls=%async_computation.16 | async-start | bytes 1966080 | tf_op jit(solution)/shard_map/reduce_scatter | solution.py:202
  568.3 95.6 %reduce-scatter.31.cloned.1.call-start = ((), (), s32[]{:S(2)}) async-start(), calls=%async_computation.23 | async-start | bytes 884736
  572.5 215.0 %all-reduce.12.cloned.1.call-start = ((), (), s32[]{:S(2)}) async-start(), calls=%async_computation.17 | async-start | bytes 6291456 | tf_op jit(solution)/shard_map/psum | solution.py:31
  632.6 200.3 %reduce-scatter.23.cloned.1.call-start = ((), (), s32[]{:S(2)}) async-start(), calls=%async_computation.19 | async-start | bytes 2654208 | tf_op jit(solution)/shard_map/reduce_scatter | solution.py:228
  638.1 241.5 %reduce-scatter.21.cloned.1.call-start = ((), (), s32[]{:S(2)}) async-start(), calls=%async_computation.18 | async-start | bytes 2654208 | tf_op jit(solution)/shard_map/reduce_scatter | solution.py:226
  642.9 275.3 %reduce-scatter.25.cloned.1.call-start = ((), (), s32[]{:S(2)}) async-start(), calls=%async_computation.20 | async-start | bytes 884736
  646.3 310.7 %reduce-scatter.29.cloned.1.call-start = ((), (), s32[]{:S(2)}) async-start(), calls=%async_computation.22 | async-start | bytes 884736
  648.1 18.8 %copy-start.46 = (f32[768]{0:T(1024)S(1)}, f32[768]{0:T(1024)}, u32[]{:S(2)}) copy-start(f32[768]{0:T(1024)} %get-tuple-element.192) | copy-start | bytes 9220
  648.1 18.8 %copy-start.48 = (f32[768]{0:T(1024)S(1)}, f32[768]{0:T(1024)}, u32[]{:S(2)}) copy-start(f32[768]{0:T(1024)} %get-tuple-element.193) | copy-start | bytes 9220
  648.1 347.5 %reduce-scatter.27.cloned.1.call-start = ((), (), s32[]{:S(2)}) async-start(), calls=%async_computation.21 | async-start | bytes 884736
  649.5 138.1 %copy-start.7 = (f32[1024,768]{1,0:T(8,128)S(1)}, f32[1024,768]{1,0:T(8,128)}, u32[]{:S(2)}) copy-start(f32[1024,768]{1,0:T(8,128)} %copy-done.5) | copy-start | bytes 9437188
  (60 other events, 253.7 us)
Sparse Core Ops, SparseCore 0:
  24.2 20.5 all-gather.4
  47.0 19.5 all-gather.6
  113.4 121.1 all-reduce.5
  249.4 120.0 all-reduce.7
  386.3 120.0 all-reduce.9
  567.7 27.1 reduce-scatter.16
  597.6 28.1 reduce-scatter.18
  629.0 34.9 reduce-scatter.30
  666.4 121.0 all-reduce.11
  791.3 41.5 reduce-scatter.22
  837.1 42.4 reduce-scatter.20
  883.2 34.9 reduce-scatter.24
  921.9 34.9 reduce-scatter.28
  960.5 34.9 reduce-scatter.26
Sparse Core Ops, SparseCore 1:
  116.3 23.9 all-gather.8
  142.6 23.9 all-gather.10
where the time goes:
time: 1010 us; the launch traced here: 1000 us
  waiting for transfers between devices  726 us (72%)
  matrix products  103 us (10%)
  blocking collectives  64.9 us (6%)
  other arithmetic  59 us (6%)
  local copies, waits for them, and re-layouts  31.5 us (3%)
  between operations  16.3 us (2%)
    psum x4, waiting for transfers between devices, head_total(): return lax.psum(partial_value, 'tp')  452 us
    unnamed x20, waiting for transfers between devices  128 us
    reduce_scatter x1, waiting for transfers between devices, body(): lax.psum_scatter(grad_up_weight, ('fsdp', 'ctx'), scatter_dimension=0, ti...  46.8 us
    reduce_scatter x1, waiting for transfers between devices, body(): lax.psum_scatter(grad_down_weight, ('fsdp', 'ctx'), scatter_dimension=1,...  42 us
    dot_general x4, matrix products, scores_of(): jnp.einsum('hqd,hkd->hqk', query_seq, key_seq, preferred_element_type=jnp...  29.7 us
    reduce_scatter x1, waiting for transfers between devices, body(): lax.psum_scatter(grad_value_part.astype(jnp.bfloat16), 'ctx', scatter_dim...  28.7 us
    psum x1, blocking collectives, body(): lax.psum((grad_query_bias, grad_value_bias, grad_output_bias, grad_first_...  25.2 us
    reduce_scatter x1, waiting for transfers between devices, body(): lax.psum_scatter(grad_key_part.astype(jnp.bfloat16), 'ctx', scatter_dimen...  20.4 us
  transfers between devices with their start and end apart: 16, of which 13 were waited for; matrix products, arithmetic and copies ran while one was open for 6% of the time, Pallas kernels for 0%

commit v1 on v0

--- a/solution.py
+++ b/solution.py
@@ -28,7 +28,7 @@
 
 
 def head_total(partial_value):
-    return lax.psum(partial_value, "tp")
+    return jnp.sum(lax.all_gather(partial_value, "tp"), axis=0)
 
 
 def head_major(flat_rows, seq_count, rows, heads_local):

time: 1010 us -> 1470 us (1.46)
  waiting for transfers between devices: 726 us -> 1160 us
  other arithmetic: 59 us -> 88.8 us
    all_gather x0 -> x4, waiting for transfers between devices: none -> 870 us  [head_total(): return jnp.sum(lax.all_gather(partial_value, 'tp'), axis=0)]
    psum x4 -> x0, waiting for transfers between devices: 452 us -> none  [head_total(): return lax.psum(partial_value, 'tp')]
    reduce_sum x2 -> x5, other arithmetic: 6.04 us -> 31.3 us  [the longest x4 30.1 us: head_total(): return jnp.sum(lax.all_gather(partial_value, 'tp'), axis=0)]
    all_gather x1, waiting for transfers between devices: 0.01 us -> 20.9 us  [body(): lax.all_gather(lowered[5], ('fsdp', 'ctx'), axis=1, tiled=True)]
  transfers between devices with their start and end apart: 16 -> 16, of which waited for: 13 -> 14; matrix products, arithmetic and copies ran while one was open for 6% -> 3% of each run, Pallas kernels for 0% -> 0%
where the time goes in v1:
time: 1470 us; the launch traced here: 1460 us
  waiting for transfers between devices  1160 us (79%)
  matrix products  99.9 us (7%)
  other arithmetic  88.8 us (6%)
  blocking collectives  64.8 us (4%)
  local copies, waits for them, and re-layouts  31.8 us (2%)
  between operations  15 us (1%)
    all_gather x4, waiting for transfers between devices, head_total(): return jnp.sum(lax.all_gather(partial_value, 'tp'), axis=0)  870 us
    unnamed x20, waiting for transfers between devices  117 us
    reduce_scatter x1, waiting for transfers between devices, body(): lax.psum_scatter(grad_up_weight, ('fsdp', 'ctx'), scatter_dimension=0, ti...  46.8 us
    reduce_scatter x1, waiting for transfers between devices, body(): lax.psum_scatter(grad_down_weight, ('fsdp', 'ctx'), scatter_dimension=1,...  37 us
    reduce_sum x4, other arithmetic, head_total(): return jnp.sum(lax.all_gather(partial_value, 'tp'), axis=0)  30.1 us
    dot_general x4, matrix products, scores_of(): jnp.einsum('hqd,hkd->hqk', query_seq, key_seq, preferred_element_type=jnp...  29.8 us
  transfers between devices with their start and end apart: 16, of which 14 were waited for; matrix products, arithmetic and copies ran while one was open for 3% of the time, Pallas kernels for 0%

profile of v1, /device:TPU:0, one launch (start us, length us, event | category | flops | bytes accessed | tf_op | source)
XLA Modules:
  0.0 1463.7 jit_solution(1919878710810640449)
XLA Ops:
  8.3 11.0 all_gather.55
  23.3 9.6 all_gather.57
  35.7 9.2 all_gather.54
  46.6 10.2 all_gather.59
  57.4 8.4 all-gather.15.cloned.1.call-done
  65.8 45.5 %while.28 = (s32[]{:T(128)}, bf16[2,3,512,64]{2,3,1,0:T(8,128)(2,1)S(1)}, f32[2,3,512,1]{2,1,3,0:T(4,128)}, f32[2,3,512,1]{2,1,3,0:T(4,128)}, s32[2,512]{1,0:T(2...) while((s32[]{:T(128)}, ...), condition=%wide.region_3.4_spmd, body=%wide.region_0.3_spmd.sunk | while | flops 844198912 | bytes 50296980 | solution.py:149
  115.9 216.9 %all-gather.21.cloned.1.call-done = f32[4096,768]{1,0:T(8,128)} async-done(((f32[1024,768]{1,0:T(8,128)}), f32[4096,768]{1,0:T(8,128)}) %all-gather.21.cloned.1.call-update) | async-done | bytes 12582928 | tf_op jit(solution)/shard_map/all_gather | solution.py:31
  347.9 9.5 all-gather.17.cloned.1.call-done
  362.9 20.9 %all-gather.19.cloned.1.call-done = bf16[768,768]{0,1:T(8,128)(2,1)} async-done(((bf16[768,96]{0,1:T(8,128)(2,1)}), bf16[768,768]{0,1:T(8,128)(2,1)}) %all-gather.19.cloned.1.call-update) | async-done | bytes 1179664 | tf_op jit(solution)/shard_map/all_gather | solution.py:129
  388.5 218.1 %all-gather.23.cloned.1.call-done = f32[4096,768]{1,0:T(8,128)} async-done(((f32[1024,768]{1,0:T(8,128)}), f32[4096,768]{1,0:T(8,128)}) %all-gather.23.cloned.1.call-update) | async-done | bytes 12582928 | tf_op jit(solution)/shard_map/all_gather | solution.py:31
  631.1 216.5 %all-gather.25.cloned.1.call-done = f32[4096,768]{1,0:T(8,128)} async-done(((f32[1024,768]{1,0:T(8,128)}), f32[4096,768]{1,0:T(8,128)}) %all-gather.25.cloned.1.call-update) | async-done | bytes 12582928 | tf_op jit(solution)/shard_map/all_gather | solution.py:31
  855.1 7.8 multiply_reduce_fusion.1
  866.8 51.1 %while.29 = (s32[]{:T(128)}, bf16[2,3,512,64]{2,3,1,0:T(8,128)(2,1)}, bf16[2,3,2048,64]{2,3,1,0:T(8,128)(2,1)}, bf16[2,3,2048,64]{2,3,1,0:T(8,128)(2,1)}, s32[2,...) while((s32[]{:T(128)}, ...), condition=%wide.region_17.18_spmd, body=%wide.region_15.17_spmd.sunk | while | flops 2046360064 | bytes 189550000 | solution.py:194
  873.3 7.7 multiply_reduce_fusion.10
  898.6 7.7 multiply_reduce_fusion.10
  920.8 23.7 %reduce-scatter.17.cloned.1.call-done = bf16[2,3,512,64]{2,3,1,0:T(8,128)(2,1)} async-done(((bf16[2,3,2048,64]{2,3,1,0:T(8,128)(2,1)}), bf16[2,3,512,64]{2,3,1,0:T(8,128)(2,1)}) %reduce-scatter.17.cloned.1.call-update) | async-done | bytes 393232 | tf_op jit(solution)/shard_map/reduce_scatter | solution.py:199
  946.7 28.7 %reduce-scatter.19.cloned.1.call-done = bf16[2,3,512,64]{2,3,1,0:T(8,128)(2,1)} async-done(((bf16[2,3,2048,64]{2,3,1,0:T(8,128)(2,1)}), bf16[2,3,512,64]{2,3,1,0:T(8,128)(2,1)}) %reduce-scatter.19.cloned.1.call-update) | async-done | bytes 393232 | tf_op jit(solution)/shard_map/reduce_scatter | solution.py:202
  982.0 218.3 %all-gather.27.cloned.1.call-done = f32[4096,768]{1,0:T(8,128)} async-done(((f32[1024,768]{1,0:T(8,128)}), f32[4096,768]{1,0:T(8,128)}) %all-gather.27.cloned.1.call-update) | async-done | bytes 12582928 | tf_op jit(solution)/shard_map/all_gather | solution.py:31
  1230.8 24.9 %all-reduce = (f32[192]{0:T(256)}, f32[192]{0:T(256)}, f32[768]{0:T(1024)}, f32[768]{0:T(1024)}, f32[768]{0:T(1024)}, /*index=5*/f32[768]{0:T(1024)}, f32[768]{0:T(1024)}, f32[768]{0:T(1024)}, f32[768]{0:T(1024)}) all-reduce(f32[192]{0:T(256)S(1)} %reduce_sum.236, ...), channel_id=1, replica_groups=mesh['fsdp'=2,'ctx'=4,'tp'=4] {'fsdp','ctx'}, use_global_device_ids=true, to_apply=%region_23.24 | all-reduce | flops 5760 | bytes 46080 | tf_op jit(solution)/shard_map/psum | solution.py:230
  1257.4 37.0 %reduce-scatter.23.cloned.1.call-done = f32[768,96]{0,1:T(8,128)} async-done(((f32[768,768]{0,1:T(8,128)}), f32[768,96]{0,1:T(8,128)}) %reduce-scatter.23.cloned.1.call-update) | async-done | bytes 294928 | tf_op jit(solution)/shard_map/reduce_scatter | solution.py:228
  1294.4 46.8 %reduce-scatter.21.cloned.1.call-done = f32[96,768]{1,0:T(8,128)} async-done(((f32[768,768]{1,0:T(8,128)}), f32[96,768]{1,0:T(8,128)}) %reduce-scatter.21.cloned.1.call-update) | async-done | bytes 294928 | tf_op jit(solution)/shard_map/reduce_scatter | solution.py:226
  1341.2 38.6 %reduce-scatter.25.cloned.1.call-done = f32[96,192]{1,0:T(8,128)} async-done(((f32[768,192]{1,0:T(8,128)}), f32[96,192]{1,0:T(8,128)}) %reduce-scatter.25.cloned.1.call-update) | async-done | bytes 73744
  1379.8 38.6 %reduce-scatter.29.cloned.1.call-done = f32[96,192]{1,0:T(8,128)} async-done(((f32[768,192]{1,0:T(8,128)}), f32[96,192]{1,0:T(8,128)}) %reduce-scatter.29.cloned.1.call-update) | async-done | bytes 73744
  1418.4 38.6 %reduce-scatter.27.cloned.1.call-done = f32[96,192]{1,0:T(8,128)} async-done(((f32[768,192]{1,0:T(8,128)}), f32[96,192]{1,0:T(8,128)}) %reduce-scatter.27.cloned.1.call-update) | async-done | bytes 73744
  (324 shorter events, 199.4 us)
Async XLA Ops:
  7.2 26.5 %copy-start.1 = (bf16[2,512,768]{2,1,0:T(8,128)(2,1)S(1)}, bf16[2,512,768]{2,1,0:T(8,128)(2,1)}, u32[]{:S(2)}) copy-start(bf16[2,512,768]{2,1,0:T(8,128)(2,1)} %param.22) | copy-start | bytes 4718596
  7.2 16.1 %copy-start.47 = (f32[96,192]{1,0:T(8,128)S(1)}, f32[96,192]{1,0:T(8,128)}, u32[]{:S(2)}) copy-start(f32[96,192]{1,0:T(8,128)} %param.27) | copy-start | bytes 221188
  7.2 26.5 %copy-start.69 = (f32[192]{0:T(256)S(1)}, f32[192]{0:T(256)}, u32[]{:S(2)}) copy-start(f32[192]{0:T(256)} %param.28) | copy-start | bytes 2308
  7.2 50.2 %all-gather.13.cloned.1.call-start = ((), (), s32[]{:S(2)}) async-start(), calls=%async_computation.8 | async-start | bytes 1966080 | tf_op jit(solution)/shard_map/all_gather | solution.py:145
  22.4 13.1 copy-start.48
  22.4 13.1 copy-start.49
  23.2 22.3 %copy-start.70 = (f32[192]{0:T(256)S(1)}, f32[192]{0:T(256)}, u32[]{:S(2)}) copy-start(f32[192]{0:T(256)} %param.25) | copy-start | bytes 2308
  23.3 42.5 %all-gather.15.cloned.1.call-start = ((), (), s32[]{:S(2)}) async-start(), calls=%async_computation.9 | async-start | bytes 1966080 | tf_op jit(solution)/shard_map/all_gather | solution.py:146
  34.6 22.2 %copy-start.38 = (s32[2,2048]{1,0:T(2,128)S(1)}, s32[2,2048]{1,0:T(2,128)}, u32[]{:S(2)}) copy-start(s32[2,2048]{1,0:T(2,128)} %param.23) | copy-start | bytes 49156
  35.5 297.3 %all-gather.21.cloned.1.call-start = ((), (), s32[]{:S(2)}) async-start(), calls=%async_computation.16 | async-start | bytes 15728640 | tf_op jit(solution)/shard_map/all_gather | solution.py:31
  114.2 243.2 %all-gather.17.cloned.1.call-start = ((), (), s32[]{:S(2)}) async-start(), calls=%async_computation.10 | async-start | bytes 1327104 | tf_op jit(solution)/shard_map/all_gather | solution.py:127
  114.9 268.9 %all-gather.19.cloned.1.call-start = ((), (), s32[]{:S(2)}) async-start(), calls=%async_computation.11 | async-start | bytes 1327104 | tf_op jit(solution)/shard_map/all_gather | solution.py:129
  115.7 490.9 %all-gather.23.cloned.1.call-start = ((), (), s32[]{:S(2)}) async-start(), calls=%async_computation.17 | async-start | bytes 15728640 | tf_op jit(solution)/shard_map/all_gather | solution.py:31
  362.9 25.3 %copy-start.75 = (bf16[1024,768]{1,0:T(8,128)(2,1)}, bf16[1024,768]{1,0:T(8,128)(2,1)S(1)}, u32[]{:S(2)}) copy-start(bf16[1024,768]{1,0:T(8,128)(2,1)S(1)} %get-tuple-element.285) | copy-start | bytes 4718596
  388.2 459.4 %all-gather.25.cloned.1.call-start = ((), (), s32[]{:S(2)}) async-start(), calls=%async_computation.18 | async-start | bytes 15728640 | tf_op jit(solution)/shard_map/all_gather | solution.py:31
  631.0 313.5 %reduce-scatter.17.cloned.1.call-start = ((), (), s32[]{:S(2)}) async-start(), calls=%async_computation.12 | async-start | bytes 1966080 | tf_op jit(solution)/shard_map/reduce_scatter | solution.py:199
  918.0 57.4 %reduce-scatter.19.cloned.1.call-start = ((), (), s32[]{:S(2)}) async-start(), calls=%async_computation.13 | async-start | bytes 1966080 | tf_op jit(solution)/shard_map/reduce_scatter | solution.py:202
  918.7 281.6 %all-gather.27.cloned.1.call-start = ((), (), s32[]{:S(2)}) async-start(), calls=%async_computation.19 | async-start | bytes 15728640 | tf_op jit(solution)/shard_map/all_gather | solution.py:31
  982.0 273.8 %reduce-scatter.31.cloned.1.call-start = ((), (), s32[]{:S(2)}) async-start(), calls=%async_computation.23 | async-start | bytes 884736
  1214.7 79.7 %reduce-scatter.23.cloned.1.call-start = ((), (), s32[]{:S(2)}) async-start(), calls=%async_computation.15 | async-start | bytes 2654208 | tf_op jit(solution)/shard_map/reduce_scatter | solution.py:228
  1219.5 121.7 %reduce-scatter.21.cloned.1.call-start = ((), (), s32[]{:S(2)}) async-start(), calls=%async_computation.14 | async-start | bytes 2654208 | tf_op jit(solution)/shard_map/reduce_scatter | solution.py:226
  1225.1 154.7 %reduce-scatter.25.cloned.1.call-start = ((), (), s32[]{:S(2)}) async-start(), calls=%async_computation.20 | async-start | bytes 884736
  1226.8 191.5 %reduce-scatter.29.cloned.1.call-start = ((), (), s32[]{:S(2)}) async-start(), calls=%async_computation.22 | async-start | bytes 884736
  1228.6 228.4 %reduce-scatter.27.cloned.1.call-start = ((), (), s32[]{:S(2)}) async-start(), calls=%async_computation.21 | async-start | bytes 884736
  (80 other events, 320.8 us)
Sparse Core Ops, SparseCore 0:
  23.4 20.5 all-gather.12
  46.1 19.6 all-gather.14
  114.3 218.4 all-gather.20
  335.1 22.2 all-gather.16
  359.7 24.0 all-gather.18
  388.3 218.1 all-gather.22
  631.1 216.3 all-gather.24
  918.1 26.3 reduce-scatter.16
  947.2 28.1 reduce-scatter.18
  982.1 218.1 all-gather.26
  1214.8 33.2 reduce-scatter.30
  1251.8 42.5 reduce-scatter.22
  1298.7 42.4 reduce-scatter.20
  1344.8 34.9 reduce-scatter.24
  1383.3 34.9 reduce-scatter.28
  1421.9 35.0 reduce-scatter.26
